TPU v7x, 32 devices: a whole 2x2x4 slice. The times are simulated.
32 devices in a mesh: gx: 4 (over y, x), gy: 8 (over z, core).
Axes of the slice: x: 2, y: 2, z: 4, core: 2. Of those that a mesh axis runs over, the one named last changes fastest.
Arguments:
- populations: float32 [19, 2, 32, 1024], P(None, None, 'gx', 'gy'), may hold values from 0.3 to 2.3, as said below
- labels: int32 [2, 32, 1024], P(None, 'gx', 'gy'), may hold values 0 or 1
- solid: int32 [2, 32, 1024], P(None, 'gx', 'gy'), may hold values 0 or 1
- rates: float32 [15], replicated, may hold values from 0.7 to 1.8
Outputs:
- final_state: float32 [2, 19, 2, 32, 1024], P(None, None, None, 'gx', 'gy')
Inputs may be any that keep to these rules, and one draw needn't show every extreme that they name: `populations`: each value is a population divided by its lattice weight, near equilibrium with a velocity of at most 0.05 a component and a density between 0.7 and 1.3, with a relative roughness of up to 0.3 a population.
All inputs are finite; a program needn't handle non-finite values. No bound on the sum of `labels` or of `solid` on one device may be relied on, other than what follows from the above.
Results may differ from a plain program's by a relative error of at most 0.0001.
Values sent between devices are 32-bit elements; how exact they have to be, the bound alone decides.
No kernel may reach another device: no remote copies, remote signals or barrier semaphores. Data moves between devices by JAX's collectives and lax.ppermute only.
A program may use at most 64 MiB of HBM per device.

v0:
```python
import jax
import jax.numpy as jnp
import numpy as np
from jax import lax
from jax.experimental import pallas as pl
from jax.experimental.pallas import tpu as pltpu
from jax.sharding import PartitionSpec as P

ITERS = 6


velocity_table = np.array(
    [
        [0, 0, 0],
        [1, 0, 0],
        [-1, 0, 0],
        [0, 1, 0],
        [0, -1, 0],
        [0, 0, 1],
        [0, 0, -1],
        [1, 1, 0],
        [-1, -1, 0],
        [1, -1, 0],
        [-1, 1, 0],
        [1, 0, 1],
        [-1, 0, -1],
        [1, 0, -1],
        [-1, 0, 1],
        [0, 1, 1],
        [0, -1, -1],
        [0, 1, -1],
        [0, -1, 1],
    ]
)
weight_table = np.array([1.0 / 3.0] + [1.0 / 18.0] * 6 + [1.0 / 36.0] * 12)
tension = 0.1
recolor_beta = 0.7
gradient_floor = 0.1


def padded_2(cells, sides, width):
    for axis, dim in sides:
        count = lax.axis_size(axis)
        head = lax.slice_in_dim(cells, 0, width, axis=dim)
        tail = lax.slice_in_dim(cells, cells.shape[dim] - width, cells.shape[dim], axis=dim)
        cells = jnp.concatenate(
            [
                lax.ppermute(tail, axis, [(i, (i + 1) % count) for i in range(count)]),
                cells,
                lax.ppermute(head, axis, [((i + 1) % count, i) for i in range(count)]),
            ],
            axis=dim,
        )
    return cells


def opposite_of(member):
    return int(np.argmax(np.all(velocity_table == -velocity_table[member], axis=1)))


def build_moments():
    float_table = velocity_table * 1.0
    first_axis = float_table[:, 0]
    second_axis = float_table[:, 1]
    depth_axis = float_table[:, 2]
    squared = first_axis**2 + second_axis**2 + depth_axis**2
    higher = 3.0 * squared - 5.0
    cubic = 5.0 * squared - 9.0
    first_diag = 3.0 * first_axis**2 - squared
    cross_diag = second_axis**2 - depth_axis**2
    listed = [
        squared * 0.0 + 1.0,
        19.0 * squared - 30.0,
        (21.0 * squared**2 - 53.0 * squared + 24.0) / 2.0,
        first_axis,
        cubic * first_axis,
        second_axis,
        cubic * second_axis,
        depth_axis,
        cubic * depth_axis,
        first_diag,
        higher * first_diag,
        cross_diag,
        higher * cross_diag,
        first_axis * second_axis,
        second_axis * depth_axis,
        first_axis * depth_axis,
        cross_diag * first_axis,
        (depth_axis**2 - first_axis**2) * second_axis,
        (first_axis**2 - second_axis**2) * depth_axis,
    ]
    return np.array(listed)


def build_placement():
    free_rows = [1, 2, 4, 6, 8] + list(range(9, 19))
    return np.eye(19)[free_rows]


def build_signs():
    return np.array([-1.0] + [1.0] * 18)


def build_lengths():
    return np.maximum(np.sqrt(np.sum((velocity_table * 1.0) ** 2, axis=1)), 1.0)


def lattice_tables():
    velocity = jnp.asarray(velocity_table, jnp.float32)
    weights = jnp.asarray(weight_table, jnp.float32)
    return (velocity, weights)


def relax_matrix(rates):
    moment_table = build_moments()
    inverse_table = moment_table.T / np.sum(moment_table**2, axis=1)[None, :]
    relaxation = jnp.dot(
        rates, jnp.asarray(build_placement(), jnp.float32), precision=lax.Precision.HIGHEST
    )
    inverse = jnp.asarray(inverse_table, jnp.float32)
    moment = jnp.asarray(moment_table, jnp.float32)
    matrix = jnp.dot(inverse * relaxation[None, :], moment, precision=lax.Precision.HIGHEST)
    weights = jnp.asarray(weight_table, jnp.float32)
    return matrix * weights[None, :] / weights[:, None]


def macroscopic(flattened):
    velocity, weights = lattice_tables()
    moment_rows = jnp.concatenate([weights[None, :], (velocity * weights[:, None]).T], axis=0)
    moments = jnp.dot(moment_rows, flattened[0], precision=lax.Precision.HIGHEST)
    red_mass = jnp.dot(weights[None, :], flattened[1], precision=lax.Precision.HIGHEST)
    return (moments, red_mass)


def collide(flattened, moments, red_mass, gradient, scaled):
    velocity, _ = lattice_tables()
    density = moments[0:1]
    velocity_field = moments[1:4] / density
    projected = jnp.dot(velocity, velocity_field, precision=lax.Precision.HIGHEST)
    squared_speed = jnp.sum(velocity_field * velocity_field, axis=0, keepdims=True)
    balance = density * (1.0 + 3.0 * projected + 4.5 * projected * projected - 1.5 * squared_speed)
    relaxed = flattened[0] - jnp.dot(
        scaled, flattened[0] - balance, precision=lax.Precision.HIGHEST
    )
    magnitude = jnp.sqrt(jnp.sum(gradient * gradient, axis=0, keepdims=True))
    bounded = jnp.maximum(magnitude, gradient_floor)
    aligned = jnp.dot(velocity, gradient, precision=lax.Precision.HIGHEST)
    sign_column = jnp.asarray(build_signs(), jnp.float32)[:, None]
    relaxed = relaxed + 0.5 * tension * (aligned * aligned / bounded - sign_column * magnitude)
    lengths = jnp.asarray(build_lengths(), jnp.float32)[:, None]
    fraction = red_mass / density
    mixing = recolor_beta * red_mass * (density - red_mass) / density
    recolored = fraction * relaxed + mixing * aligned / (lengths * bounded)
    return jnp.stack([relaxed, recolored])


def gradient_local(padded_phase, height, breadth):
    components = [
        jnp.zeros((padded_phase.shape[0], height, breadth), jnp.float32) for _ in range(3)
    ]
    for member in range(1, 19):
        along_first, along_second, along_depth = (int(value) for value in velocity_table[member])
        window = padded_phase[
            :,
            1 + along_first : 1 + along_first + height,
            1 + along_second : 1 + along_second + breadth,
        ]
        shifted = jnp.roll(window, -along_depth, axis=0)
        factor = 3.0 * float(weight_table[member])
        for axis_number, along in enumerate((along_first, along_second, along_depth)):
            if along != 0:
                components[axis_number] = components[axis_number] + factor * along * shifted
    return jnp.stack(components)


def stream_local(padded, collided, current, solid_pad, blocked, height, breadth):
    results = []
    for member in range(19):
        along_first, along_second, along_depth = (int(value) for value in velocity_table[member])
        window = padded[
            :,
            member,
            :,
            1 - along_first : 1 - along_first + height,
            1 - along_second : 1 - along_second + breadth,
        ]
        shifted = jnp.roll(window, along_depth, axis=1)
        rock_window = solid_pad[
            :,
            1 - along_first : 1 - along_first + height,
            1 - along_second : 1 - along_second + breadth,
        ]
        source_rock = jnp.roll(rock_window, along_depth, axis=0)
        bounced = collided[:, opposite_of(member)]
        pulled = jnp.where(source_rock[None], bounced, shifted)
        results.append(jnp.where(blocked[None], current[:, member], pulled))
    return jnp.stack(results, axis=1)


def body_plain(populations, labels, solid, rates):
    scaled = relax_matrix(rates)
    red_part = labels.astype(jnp.float32)[None] * populations
    current = jnp.stack([populations, red_part])
    height = populations.shape[2]
    breadth = populations.shape[3]
    blocked = solid > 0
    grid_shape = current.shape
    solid_pad = padded_2(solid, (("gx", 1), ("gy", 2)), 1) > 0
    for _ in range(ITERS):
        flattened = current.reshape(2, 19, -1)
        moments, red_mass = macroscopic(flattened)
        phase_field = ((2.0 * red_mass - moments[0:1]) / moments[0:1]).reshape(grid_shape[2:])
        padded_phase = padded_2(phase_field, (("gx", 1), ("gy", 2)), 1)
        gradient = gradient_local(padded_phase, height, breadth).reshape(3, -1)
        collided = collide(flattened, moments, red_mass, gradient, scaled).reshape(grid_shape)
        padded = padded_2(collided, (("gx", 3), ("gy", 4)), 1)
        current = stream_local(padded, collided, current, solid_pad, blocked, height, breadth)
    return current


SUB = 8
LANES = 128
HALF = LANES // 2
SLOT = 16
REACH = 2 * ITERS
INSIDE = 32 - REACH
TURN = 2 * REACH
GROUP = 4
SIDE_COUNT = -(-21 // GROUP)
ROWS = 5 * SUB
FIRST = 2 * SUB
LAST_ROWS = 2 * SUB
PAIRS = [(m, opposite_of(m)) for m in range(1, 19) if m < opposite_of(m)]


def lane_ids(shape):
    return lax.broadcasted_iota(jnp.int32, shape, len(shape) - 1)


def within(shape, *spans):
    ids = lane_ids(shape)
    mask = None
    for first, last in spans:
        for shift in (0, HALF):
            low, high = (first + shift) % LANES, (last + shift) % LANES
            part = (ids >= low) & (ids < high) if low < high else (ids >= low) | (ids < high)
            mask = part if mask is None else mask | part
    return mask


def lane_roll(value, amount):
    return pltpu.roll(value, amount % LANES, axis=value.ndim - 1)


def moved_apart(planes, swap, along):
    if swap:
        planes = planes[::-1]
    return [lane_roll(p, along) for p in planes] if along else planes


def moved_zone(planes, swap, along):
    amount = (HALF if swap else 0) + along
    return [lane_roll(p, amount) for p in planes] if amount else planes


def moved_joined(planes, swap, along):
    first, second, side = planes
    if swap:
        first, second = second, first
    amount = (HALF if swap else 0) + along
    if amount:
        first, second, side = (lane_roll(p, amount) for p in (first, second, side))
    if along:
        ids = lane_ids(first.shape)
        edge = 0 if along > 0 else LANES - 1
        at_first = ids == edge
        at_second = ids == (edge + HALF) % LANES
        first, second, side = (
            jnp.where(at_first, side, first),
            jnp.where(at_second, side, second),
            jnp.where(at_first, first, jnp.where(at_second, second, side)),
        )
    return first, second, side


def gather_kernel(pop_ref, lab_ref, sol_ref, main, inner_ref, outer_ref):
    for member in range(19):
        for at in range(2):
            main[2 * member + at] = pop_ref[member, at]
    for at in range(2):
        main[38 + at] = lab_ref[at].astype(jnp.float32)
        main[40 + at] = sol_ref[at].astype(jnp.float32)
    even = lax.axis_index("gy") % 2 == 0
    low = lane_ids((SUB, LANES)) < HALF
    left_spans = [(SLOT * k, SLOT * k + REACH) for k in range(GROUP)]
    lefts = [within((SUB, LANES), span) for span in left_spans]
    rights = [within((SUB, LANES), (first - REACH, last - REACH)) for first, last in left_spans]
    deep_left = ~low
    deep_rights = [
        (lane_ids((SUB, LANES)) >= HALF - REACH + SLOT * k)
        & (lane_ids((SUB, LANES)) < LANES - REACH + SLOT * k)
        for k in range(GROUP)
    ]
    for index in range(SIDE_COUNT):
        left_all = right_all = None
        for k in range(min(GROUP, 21 - GROUP * index)):
            member = GROUP * index + k
            shallow = main[2 * member]
            if k:
                shallow = lane_roll(shallow, SLOT * k)
            deep = lane_roll(main[2 * member + 1], HALF + SLOT * k)
            left = jnp.where(deep_left, deep, shallow)
            right = jnp.where(deep_rights[k], deep, shallow)
            left_all = left if k == 0 else jnp.where(lefts[k], left, left_all)
            right_all = right if k == 0 else jnp.where(rights[k], right, right_all)
        inner_ref[index] = jnp.where(even, right_all, left_all)
        outer_ref[index] = jnp.where(even, left_all, right_all)


def weighted_sum(values):
    axis = values[1]
    for q in range(2, 7):
        axis = axis + values[q]
    diag = values[7]
    for q in range(8, 19):
        diag = diag + values[q]
    return 12.0 * values[0] + 2.0 * axis + diag


class Stepper:
    pass


def make_stepper(refs, moved, rates_ref):
    state, after, phase, total, inverse, red, mask, rock = refs
    count = state.shape[1]
    stepper = Stepper()
    norms = np.sum(build_moments() ** 2, axis=1)
    free = [1, 2, 4, 6, 8] + list(range(9, 19))
    rate = {row: rates_ref[k] * float(1.0 / norms[row]) for k, row in enumerate(free)}

    def put_macro(j, rows, density, reds, where=None):
        inv = 1.0 / density
        values = ((total, density), (inverse, inv), (red, reds), (phase, (2.0 * reds - density) * inv))
        for ref, value in values:
            if where is None:
                ref[j, rows, :] = value
            else:
                pltpu.store(ref.at[j, rows, :], value, mask=where)

    def make_masks(base):
        for member in range(1, 19):
            a, b, c = (int(v) for v in velocity_table[member])
            planes = moved([rock[j, pl.ds(base - a, SUB), :] for j in range(count)], c % 2 == 1, b)
            for j in range(count):
                mask[member - 1, j, pl.ds(base, SUB), :] = planes[j]

    axis_a9 = rate[9] + 4.0 * rate[10]
    cross_9 = rate[9] - 2.0 * rate[10]
    diag_9 = rate[9] + rate[10]
    axis_a11 = rate[11] + 4.0 * rate[12]
    cross_11 = rate[11] - 2.0 * rate[12]
    diag_11 = rate[11] + rate[12]

    def gradient_planes(base):
        before = [phase[j, pl.ds(base - 1, SUB), :] for j in range(count)]
        here = [phase[j, pl.ds(base, SUB), :] for j in range(count)]
        behind = [phase[j, pl.ds(base + 1, SUB), :] for j in range(count)]
        slope = [p - m for p, m in zip(behind, before)]
        both = [p + m for p, m in zip(behind, before)]
        rim = [2.0 * h + s for h, s in zip(here, both)]
        slope_up, slope_down = moved(slope, False, -1), moved(slope, False, 1)
        slope_deep = moved(slope, True, 0)
        here_up, here_down = moved(here, False, -1), moved(here, False, 1)
        here_deep = moved(here, True, 0)
        rim_y = [r + (d + d) for r, d in zip(rim, here_deep)]
        rim_up, rim_down = moved(rim_y, False, -1), moved(rim_y, False, 1)
        rim_z = [r + (u + d) for r, u, d in zip(rim, here_up, here_down)]
        deeper, shallower = moved(rim_z, True, 0), moved(rim_z, True, 0)
        scale = 1.0 / 12.0
        return [
            (
                scale * (2.0 * slope[j] + (slope_up[j] + slope_down[j]) + (slope_deep[j] + slope_deep[j])),
                scale * (rim_up[j] - rim_down[j]),
                scale * (deeper[j] - shallower[j]),
            )
            for j in range(count)
        ]

    def collide_plane(j, base, grads):
        rows = pl.ds(base, SUB)
        gx, gy, gz = grads
        density, inv, reds = total[j, rows, :], inverse[j, rows, :], red[j, rows, :]
        value = [state[q, j, rows, :] for q in range(19)]
        even = {p: value[p] + value[o] for p, o in PAIRS}
        odd = {p: value[p] - value[o] for p, o in PAIRS}
        ex, ey, ez = 2.0 * even[1], 2.0 * even[3], 2.0 * even[5]
        ox, oy, oz = 2.0 * odd[1], 2.0 * odd[3], 2.0 * odd[5]
        pxy, pxz, pyz = even[7] + even[9], even[11] + even[13], even[15] + even[17]
        rxy, rxz, ryz = even[7] - even[9], even[11] - even[13], even[15] - even[17]
        x_xy, y_xy = odd[7] + odd[9], odd[7] - odd[9]
        x_xz, z_xz = odd[11] + odd[13], odd[11] - odd[13]
        y_yz, z_yz = odd[15] + odd[17], odd[15] - odd[17]
        tx, ty, tz = x_xy + x_xz, y_xy + y_yz, z_xz + z_yz
        jx, jy, jz = ox + tx, oy + ty, oz + tz
        ux, uy, uz = jx * inv, jy * inv, jz * inv
        xx, yy, zz = jx * ux, jy * uy, jz * uz
        square = xx + yy + zz
        sum_axis = ex + ey + ez
        sum_diag = pxy + pxz + pyz
        rest = 12.0 * value[0]
        d_energy = 8.0 * sum_diag - 11.0 * sum_axis - 30.0 * rest + 11.0 * density - 19.0 * square
        d_second = sum_diag - 4.0 * sum_axis + 12.0 * rest - 3.0 * density + 5.5 * square
        flat_x = 1.5 * xx - 0.5 * square
        flat_w = 0.5 * (yy - zz)
        a9 = 3.0 * ex - sum_axis - flat_x
        b9 = sum_diag - 3.0 * pyz - flat_x
        a11 = ey - ez - flat_w
        b11 = pxy - pxz - flat_w
        axis_x = (0.5 * axis_a9) * a9 + (0.5 * cross_9) * b9
        diag_x = cross_9 * a9 + diag_9 * b9
        axis_w = (0.5 * axis_a11) * a11 + (0.5 * cross_11) * b11
        diag_w = cross_11 * a11 + diag_11 * b11
        norm2 = gx * gx + gy * gy + gz * gz
        size = jnp.sqrt(norm2)
        inv_bound = 1.0 / jnp.maximum(size, gradient_floor)
        pull = (0.5 * tension) * size
        push = (0.5 * tension) * inv_bound
        iso_axis = (-5.5 * rate[1]) * d_energy - (2.0 * rate[2]) * d_second + pull
        iso_diag = (8.0 * rate[1]) * d_energy + rate[2] * d_second + pull
        iso_rest = (-2.5 * rate[1]) * d_energy + rate[2] * d_second - pull
        out_even = {
            1: iso_axis + 2.0 * axis_x,
            3: iso_axis - axis_x + axis_w,
            5: iso_axis - axis_x - axis_w,
        }
        dxy = iso_diag + diag_x + diag_w
        dxz = iso_diag + diag_x - diag_w
        dyz = iso_diag - 2.0 * diag_x
        sxy = rate[13] * (rxy - jx * uy)
        syz = rate[14] * (ryz - jy * uz)
        sxz = rate[15] * (rxz - jx * uz)
        out_even.update(
            {7: dxy + sxy, 9: dxy - sxy, 11: dxz + sxz, 13: dxz - sxz, 15: dyz + syz, 17: dyz - syz}
        )
        third = 2.0 / 3.0
        qx = rate[4] * (tx - 4.0 * ox + third * jx)
        qy = rate[6] * (ty - 4.0 * oy + third * jy)
        qz = rate[8] * (tz - 4.0 * oz + third * jz)
        mx = rate[16] * (x_xy - x_xz)
        my = rate[17] * (y_yz - y_xy)
        mz = rate[18] * (z_xz - z_yz)
        fx, fy = qx + mx, qy - my
        hx, hz = qx - mx, qz + mz
        ky, kz = qy + my, qz - mz
        out_odd = {
            1: -2.0 * qx,
            3: -2.0 * qy,
            5: -2.0 * qz,
            7: fx + fy,
            9: fx - fy,
            11: hx + hz,
            13: hx - hz,
            15: ky + kz,
            17: ky - kz,
        }
        along = {
            1: gx,
            3: gy,
            5: gz,
            7: gx + gy,
            9: gx - gy,
            11: gx + gz,
            13: gx - gz,
            15: gy + gz,
            17: gy - gz,
        }
        fraction = reds * inv
        mixing = (recolor_beta / 36.0) * reds * (1.0 - fraction)
        mix_axis = mixing * inv_bound
        mix_diag = mix_axis * float(1.0 / np.sqrt(2.0))
        relaxed = value[0] - iso_rest
        after[0, j, rows, :] = relaxed
        after[19, j, rows, :] = fraction * relaxed
        for p, o in PAIRS:
            steady = out_even[p] - (along[p] * along[p]) * push
            mixed = along[p] * (mix_axis if p < 7 else mix_diag)
            forth = value[p] - (steady + out_odd[p])
            reverse = value[o] - (steady - out_odd[p])
            after[p, j, rows, :] = forth
            after[o, j, rows, :] = reverse
            after[19 + p, j, rows, :] = fraction * forth + mixed
            after[19 + o, j, rows, :] = fraction * reverse - mixed

    def collide_rows(base):
        grads = gradient_planes(base)
        for j in range(count):
            collide_plane(j, base, grads[j])

    def stream_rows(base):
        rows = pl.ds(base, SUB)
        fluid = [rock[j, rows, :] < 0.5 for j in range(count)]
        sums = [[[] for _ in range(count)] for _ in range(2)]
        for q in range(19):
            a, b, c = (int(v) for v in velocity_table[q])
            back_rows = pl.ds(base - a, SUB)
            if q > 0:
                hits = [mask[q - 1, j, rows, :] > 0.5 for j in range(count)]
            for s in range(2):
                planes = [after[19 * s + q, j, back_rows, :] for j in range(count)]
                if q > 0:
                    planes = moved(planes, c % 2 == 1, b)
                    other = 19 * s + opposite_of(q)
                    planes = [
                        jnp.where(hits[j], after[other, j, rows, :], planes[j]) for j in range(count)
                    ]
                for j in range(count):
                    pltpu.store(state.at[19 * s + q, j, rows, :], planes[j], mask=fluid[j])
                    sums[s][j].append(planes[j])
        for j in range(count):
            put_macro(j, rows, weighted_sum(sums[0][j]), weighted_sum(sums[1][j]), fluid[j])

    def fill(values, labels, rocks, rows):
        sums = [[] for _ in range(count)]
        for member in range(19):
            planes = values(member)
            for j in range(count):
                state[member, j, rows, :] = planes[j]
                state[19 + member, j, rows, :] = labels[j] * planes[j]
                sums[j].append(planes[j])
        for j in range(count):
            rock[j, rows, :] = rocks[j]
            density = weighted_sum(sums[j])
            put_macro(j, rows, density, labels[j] * density)

    def run_early():
        rows_loop(FIRST - REACH + 2, SUB + 2 * REACH - 4, make_masks)
        for iteration in range(ITERS - 1):
            width = REACH - 2 * iteration
            rows_loop(FIRST - width + 1, SUB + 2 * width - 2, collide_rows)
            rows_loop(FIRST - width + 2, SUB + 2 * width - 4, stream_rows)

    stepper.put_macro, stepper.fill, stepper.run_early = put_macro, fill, run_early
    stepper.collide_rows = collide_rows
    return stepper


def rows_loop(start, count, run):
    for index in range(-(-count // SUB)):
        run(start + index * SUB)


def tile_places(spots):
    return [pl.ds(pl.multiple_of(spot * SUB, SUB), SUB) for spot in spots]


def early_kernel(mains, rates_ref, own_ref, rock_ref, zone_ref, *scratch):
    state, rock = scratch[0], scratch[-1]
    stepper = make_stepper(scratch, moved_apart, rates_ref)
    shape = (SUB, LANES)
    ids = lane_ids(shape)
    deep = (ids >= HALF - INSIDE) & (ids < LANES - INSIDE)
    left = within(shape, (TURN, TURN + INSIDE))
    for source, (main, spots) in enumerate(zip(mains, tile_spots(lax.axis_index("gx"), len(mains)))):
        for rows in tile_places(spots):
            labels = [main[38], main[39]]
            rocks = [main[40], main[41]]
            stepper.fill(lambda member: [main[2 * member], main[2 * member + 1]], labels, rocks, rows)
        for member in range(21):
            shallow, below = main[2 * member], main[2 * member + 1]
            right_part = jnp.where(deep, lane_roll(below, HALF), shallow)
            left_part = jnp.where(ids < HALF, lane_roll(shallow, TURN), lane_roll(below, HALF + TURN))
            zone_ref[source * 21 + member] = jnp.where(left, left_part, right_part)
    stepper.run_early()
    for tile in range(LAST_ROWS // SUB):
        rows, here = pl.ds(tile * SUB, SUB), pl.ds(FIRST - 2 + tile * SUB, SUB)
        for q in range(38):
            own_ref[q, 0, rows, :] = state[q, 0, here, :]
            own_ref[q, 1, rows, :] = lane_roll(state[q, 1, here, :], HALF)
        rock_ref[0, rows, :] = rock[0, here, :]
        rock_ref[1, rows, :] = lane_roll(rock[1, here, :], HALF)


def late_kernel(sides, own_ref, rock_ref, zone_ref, rates_ref, out_ref, *scratch):
    zone_scratch, last_scratch = scratch[:8], scratch[8:]
    shape = (SUB, LANES)
    ids = lane_ids(shape)
    sources = zone_ref.shape[0] // 21
    even = lax.axis_index("gy") % 2 == 0
    zone = make_stepper(zone_scratch, moved_zone, rates_ref)
    is_ahead = within(shape, (0, REACH))
    is_behind = within(shape, (REACH, TURN))
    for source, spots in enumerate(tile_spots(lax.axis_index("gx"), sources)):
        planes = []
        for member in range(21):
            index, k = member // GROUP, member % GROUP
            if k == 0:
                inner, outer = sides[source][index], sides[source][SIDE_COUNT + index]
                ahead_pack = jnp.where(even, inner, outer)
                behind_pack = jnp.where(even, outer, inner)
            ahead = lane_roll(ahead_pack, -SLOT * k) if k else ahead_pack
            behind = lane_roll(behind_pack, TURN - SLOT * k)
            own = zone_ref[source * 21 + member]
            planes.append(jnp.where(is_ahead, ahead, jnp.where(is_behind, behind, own)))
        for rows in tile_places(spots):
            zone.fill(lambda member: [planes[member]], [planes[19]], [planes[20]], rows)
    zone.run_early()

    last = make_stepper(last_scratch, moved_joined, rates_ref)
    state, after, rock = last_scratch[0], last_scratch[1], last_scratch[-1]
    lost = 2 * (ITERS - 1)
    from_left = [(ids >= at) & (ids < at + lost) for at in (0, HALF)]
    from_right = [(ids >= at - lost) & (ids < at) for at in (LANES, HALF)]
    right_side = within(shape, (0, 32))
    for tile in range(LAST_ROWS // SUB):
        rows, here = pl.ds(tile * SUB, SUB), pl.ds(FIRST - 2 + tile * SUB, SUB)

        def joined(around, own):
            turned = lane_roll(around, -TURN)
            planes = [
                jnp.where(from_left[j], turned, jnp.where(from_right[j], around, own[j]))
                for j in range(2)
            ]
            return planes + [jnp.where(right_side, around, turned)]

        planes = joined(zone_scratch[-1][0, here, :], [rock_ref[j, rows, :] for j in range(2)])
        for j in range(3):
            rock[j, rows, :] = planes[j]
        sums = [[[] for _ in range(3)] for _ in range(2)]
        for q in range(38):
            own = [own_ref[q, j, rows, :] for j in range(2)]
            planes = joined(zone_scratch[0][q, 0, here, :], own)
            for j in range(3):
                state[q, j, rows, :] = planes[j]
                sums[q // 19][j].append(planes[j])
        for j in range(3):
            last.put_macro(j, rows, weighted_sum(sums[0][j]), weighted_sum(sums[1][j]))
    rows_loop(1, SUB + 2, last.collide_rows)
    rows = pl.ds(2, SUB)
    fluid = [rock[j, rows, :] < 0.5 for j in range(2)]
    for q in range(19):
        a, b, c = (int(v) for v in velocity_table[q])
        back_rows = pl.ds(2 - a, SUB)
        hits = moved_joined([rock[j, back_rows, :] for j in range(3)], c % 2 == 1, b)
        for s in range(2):
            planes = [after[19 * s + q, j, back_rows, :] for j in range(3)]
            planes = moved_joined(planes, c % 2 == 1, b)
            for j in range(2):
                value = planes[j]
                if q > 0:
                    bounced = after[19 * s + opposite_of(q), j, rows, :]
                    value = jnp.where(hits[j] > 0.5, bounced, value)
                value = jnp.where(fluid[j], value, state[19 * s + q, j, rows, :])
                out_ref[s, q, j] = lane_roll(value, HALF) if j else value


def next_pairs(count):
    return [i ^ 1 for i in range(count)]


def other_pairs(count):
    return [(i + 1 if i % 2 else i - 1) % count for i in range(count)]


def far_pairs(count):
    first = [i + 2 if i % 4 < 2 else i - 2 for i in range(count)]
    second = [(i - 2 if i % 4 < 2 else i + 2) % count for i in range(count)]
    return [first] if first == second else [first, second]


def tile_spots(index, count):
    odd = index % 2
    late = (index // 2) % 2
    near = [(2,), (3 - 2 * odd,), (1 + 2 * odd,)]
    if count == 4:
        return near + [(0, 4)]
    return near + [(4 - 4 * late,), (4 * late,)]


def swapped(value, axis, partners):
    return lax.ppermute(value, axis, list(enumerate(partners)))


def vmem_call(kernel, out_shapes, args, rates=None, scratch=()):
    vmem = pl.BlockSpec(memory_space=pltpu.VMEM)
    specs = [vmem] * len(args)
    args = [pltpu.with_memory_space_constraint(arg, pltpu.VMEM) for arg in args]
    if rates is not None:
        specs.append(pl.BlockSpec(memory_space=pltpu.SMEM))
        args.append(rates)
    return pl.pallas_call(kernel, out_shape=out_shapes, in_specs=specs, scratch_shapes=scratch)(*args)


def scratch_planes(count, rows):
    plane = pltpu.VMEM((count, rows, LANES), jnp.float32)
    full = pltpu.VMEM((38, count, rows, LANES), jnp.float32)
    masks = pltpu.VMEM((18, count, rows, LANES), jnp.float32)
    return [full, full, plane, plane, plane, plane, masks, plane]


def body_deep(populations, labels, solid, rates):
    high, wide = lax.axis_size("gx"), lax.axis_size("gy")
    patterns = [next_pairs(high), other_pairs(high)] + far_pairs(high)
    number = 1 + len(patterns)

    def planes(*shape):
        return pltpu.VMEM(shape + (LANES,), jnp.float32)

    def early(*refs):
        early_kernel(refs[:number], *refs[number:])

    def late(*refs):
        late_kernel(refs[:number], *refs[number:])

    border = planes(SIDE_COUNT, SUB)
    main, inner, outer = pl.pallas_call(gather_kernel, out_shape=(planes(42, SUB), border, border))(
        populations, labels, solid
    )
    mains = [main] + [swapped(main, "gx", partners) for partners in patterns]
    outer = swapped(outer, "gy", other_pairs(wide))
    inner = swapped(inner, "gy", next_pairs(wide))
    side = jnp.concatenate([inner, outer], axis=0)
    sides = [side] + [swapped(side, "gx", partners) for partners in patterns]
    kept = (planes(38, 2, LAST_ROWS), planes(2, LAST_ROWS), planes(number * 21, SUB))
    own, rock, zone = vmem_call(early, kept, mains, rates, scratch_planes(2, ROWS))
    return vmem_call(
        late,
        jax.ShapeDtypeStruct((2,) + populations.shape, jnp.float32),
        sides + [own, rock, zone],
        rates,
        scratch_planes(1, ROWS) + scratch_planes(3, LAST_ROWS + SUB),
    )


def body(populations, labels, solid, rates):
    depth, height, breadth = populations.shape[1:]
    fits = (depth, height, breadth) == (2, SUB, LANES)
    fits = fits and lax.axis_size("gx") % 4 == 0 and lax.axis_size("gy") % 2 == 0
    if fits and REACH + 2 < SLOT and HALF == 2 * (REACH + INSIDE):
        return body_deep(populations, labels, solid, rates)
    return body_plain(populations, labels, solid, rates)


def solution(mesh):
    return jax.shard_map(
        body,
        mesh=mesh,
        in_specs=(P(None, None, "gx", "gy"), P(None, "gx", "gy"), P(None, "gx", "gy"), P()),
        out_specs=P(None, None, None, "gx", "gy"),
        check_vma=False,
    )
```

profile of v0, /device:TPU:0, one launch (start us, length us, event | category | flops | bytes accessed | tf_op | source)
XLA Modules:
  0.0 24.4 jit_solution(17733238502891885128)
XLA Ops:
  0.0 1.0 %shard_map.46 = (f32[42,8,128]{2,1,0:T(8,128)S(1)}, f32[6,8,128]{2,1,0:T(8,128)S(1)}, f32[6,8,128]{2,1,0:T(8,128)S(1)}) custom-call(f32[19,2,8,128]{3,2,1,0:T(8,128)} %pop_ref.1, s32[2,8,128]{2,1,0:T(8,128)} %lab_ref.1, s32[2,8,128]{2,1,0:T(8,128)} %sol_ref.1), custom_call_target="tpu_custom_call" | custom-call | tf_op jit(solution)/shard_map/pallas_call | solution.py:716
  1.0 0.6 %collective-permute-start = (f32[6,8,128]{2,1,0:T(8,128)S(1)}, f32[6,8,128]{2,1,0:T(8,128)S(1)}, u32[]{:S(2)}, u32[]{:S(2)}) collective-permute-start(f32[6,8,128]{2,1,0:T(8,128)S(1)} %get-tuple-element.11), channel_id=1, source_target_pairs={{0,1},{1,0},{2,3},{3,2},{4,5},{5,4},{6,7},{7,6},{8,9},{9,8},{10,11... | collective-permute-start | bytes 73736 | tf_op jit(solution)/shard_map/ppermute | solution.py:681
  1.6 2.6 %collective-permute-start.5 = (f32[42,8,128]{2,1,0:T(8,128)S(1)}, f32[42,8,128]{2,1,0:T(8,128)S(1)}, u32[]{:S(2)}, u32[]{:S(2)}) collective-permute-start(f32[42,8,128]{2,1,0:T(8,128)S(1)} %get-tuple-element.13.refs_0_), channel_id=1, source_target_pairs={{0,8},{8,0},{16,24},{24,16},{1,9},{9,1},{17,25},{25,17},{2,10},{10... | collective-permute-start | bytes 516104 | tf_op jit(solution)/shard_map/ppermute | solution.py:681
  4.2 1.5 %collective-permute-start.6 = (f32[42,8,128]{2,1,0:T(8,128)S(1)}, f32[42,8,128]{2,1,0:T(8,128)S(1)}, u32[]{:S(2)}, u32[]{:S(2)}) collective-permute-start(f32[42,8,128]{2,1,0:T(8,128)S(1)} %get-tuple-element.13.refs_0_), channel_id=1, source_target_pairs={{0,24},{8,16},{16,8},{24,0},{1,25},{9,17},{17,9},{25,1},{2,26},{10... | collective-permute-start | bytes 516104 | tf_op jit(solution)/shard_map/ppermute | solution.py:681
  5.6 0.1 collective-permute-start.7
  5.7 3.3 %collective-permute-start.1 = (f32[6,8,128]{2,1,0:T(8,128)S(1)}, f32[6,8,128]{2,1,0:T(8,128)S(1)}, u32[]{:S(2)}, u32[]{:S(2)}) collective-permute-start(f32[6,8,128]{2,1,0:T(8,128)S(1)} %get-tuple-element.12), channel_id=1, source_target_pairs={{0,7},{1,2},{2,1},{3,4},{4,3},{5,6},{6,5},{7,0},{8,15},{9,10},{10,... | collective-permute-start | bytes 73736 | tf_op jit(solution)/shard_map/ppermute | solution.py:681
  8.9 0.0 collective-permute-done
  9.0 1.9 %collective-permute-done.1 = f32[6,8,128]{2,1,0:T(8,128)S(1)} collective-permute-done((f32[6,8,128]{2,1,0:T(8,128)S(1)}, f32[6,8,128]{2,1,0:T(8,128)S(1)}, u32[]{:S(2)}, u32[]{:S(2)}) %collective-permute-start.1) | collective-permute-done | bytes 24608 | tf_op jit(solution)/shard_map/ppermute | solution.py:681
  10.8 1.9 %collective-permute-start.2 = (f32[12,8,128]{2,1,0:T(8,128)S(1)}, f32[12,8,128]{2,1,0:T(8,128)S(1)}, u32[]{:S(2)}, u32[]{:S(2)}) collective-permute-start(f32[12,8,128]{2,1,0:T(8,128)S(1)} %constant_dynamic-update-slice_fusion.refs_0_), channel_id=1, source_target_pairs={{0,8},{8,0},{16,24},{24,16},{1,9},{9,1},{17,25},{25,17},{2,10},{10... | collective-permute-start | bytes 147464 | tf_op jit(solution)/shard_map/ppermute | solution.py:681
  12.7 1.5 %collective-permute-start.3 = (f32[12,8,128]{2,1,0:T(8,128)S(1)}, f32[12,8,128]{2,1,0:T(8,128)S(1)}, u32[]{:S(2)}, u32[]{:S(2)}) collective-permute-start(f32[12,8,128]{2,1,0:T(8,128)S(1)} %constant_dynamic-update-slice_fusion.refs_0_), channel_id=1, source_target_pairs={{0,24},{8,16},{16,8},{24,0},{1,25},{9,17},{17,9},{25,1},{2,26},{10... | collective-permute-start | bytes 147464 | tf_op jit(solution)/shard_map/ppermute | solution.py:681
  14.2 0.0 collective-permute-done.5.refs_1_
  14.2 0.1 collective-permute-start.4
  14.3 0.3 %collective-permute-done.6.refs_2_ = f32[42,8,128]{2,1,0:T(8,128)S(1)} collective-permute-done((f32[42,8,128]{2,1,0:T(8,128)S(1)}, f32[42,8,128]{2,1,0:T(8,128)S(1)}, u32[]{:S(2)}, u32[]{:S(2)}) %collective-permute-start.6) | collective-permute-done | bytes 172064 | tf_op jit(solution)/shard_map/ppermute | solution.py:681
  14.6 1.9 %collective-permute-done.7.refs_3_ = f32[42,8,128]{2,1,0:T(8,128)S(1)} collective-permute-done((f32[42,8,128]{2,1,0:T(8,128)S(1)}, f32[42,8,128]{2,1,0:T(8,128)S(1)}, u32[]{:S(2)}, u32[]{:S(2)}) %collective-permute-start.7) | collective-permute-done | bytes 172064 | tf_op jit(solution)/shard_map/ppermute | solution.py:681
  16.5 3.5 %shard_map.47 = (f32[38,2,16,128]{3,2,1,0:T(8,128)S(1)}, f32[2,16,128]{2,1,0:T(8,128)S(1)}, f32[84,8,128]{2,1,0:T(8,128)S(1)}) custom-call(f32[42,8,128]{2,1,0:T(8,128)S(1)} %get-tuple-element.13.refs_0_, f32[42,8,128]{2,1,0:T(8,128)S(1)} %collective-permute-done.5.refs_1_, f32[42,8,128]{2,1,0:T(8,128)S(1)} %collective-permute-done.6.refs_2_, ...), custom_call_target="tpu_custom_call" | custom-call | tf_op jit(solution)/shard_map/pallas_call | solution.py:691
  20.0 0.0 collective-permute-done.2.refs_1_
  20.1 0.0 collective-permute-done.3.refs_2_
  20.1 0.0 collective-permute-done.4.refs_3_
  20.1 4.4 %shard_map.48 = f32[2,19,2,8,128]{4,3,2,1,0:T(8,128)} custom-call(f32[12,8,128]{2,1,0:T(8,128)S(1)} %constant_dynamic-update-slice_fusion.refs_0_, f32[12,8,128]{2,1,0:T(8,128)S(1)} %collective-permute-done.2.refs_1_, f32[12,8,128]{2,1,0:T(8,128)S(1)} %collective-permute-done.3.refs_2_, f32[12,8,128]{2,1,0:T(8,128)S(1)} %collective-permute-done.4.refs_3_, ...), custom_call_target="tpu_custom_call" | custom-call | tf_op jit(solution)/shard_map/pallas_call | solution.py:691
  (2 shorter events, 0.0 us)
Async XLA Ops:
  1.0 7.9 %collective-permute-start = (f32[6,8,128]{2,1,0:T(8,128)S(1)}, f32[6,8,128]{2,1,0:T(8,128)S(1)}, u32[]{:S(2)}, u32[]{:S(2)}) collective-permute-start(f32[6,8,128]{2,1,0:T(8,128)S(1)} %get-tuple-element.11), channel_id=1, source_target_pairs={{0,1},{1,0},{2,3},{3,2},{4,5},{5,4},{6,7},{7,6},{8,9},{9,8},{10,11... | collective-permute-start | bytes 73736 | tf_op jit(solution)/shard_map/ppermute | solution.py:681
  1.6 12.6 %collective-permute-start.5 = (f32[42,8,128]{2,1,0:T(8,128)S(1)}, f32[42,8,128]{2,1,0:T(8,128)S(1)}, u32[]{:S(2)}, u32[]{:S(2)}) collective-permute-start(f32[42,8,128]{2,1,0:T(8,128)S(1)} %get-tuple-element.13.refs_0_), channel_id=1, source_target_pairs={{0,8},{8,0},{16,24},{24,16},{1,9},{9,1},{17,25},{25,17},{2,10},{10... | collective-permute-start | bytes 516104 | tf_op jit(solution)/shard_map/ppermute | solution.py:681
  4.2 10.4 %collective-permute-start.6 = (f32[42,8,128]{2,1,0:T(8,128)S(1)}, f32[42,8,128]{2,1,0:T(8,128)S(1)}, u32[]{:S(2)}, u32[]{:S(2)}) collective-permute-start(f32[42,8,128]{2,1,0:T(8,128)S(1)} %get-tuple-element.13.refs_0_), channel_id=1, source_target_pairs={{0,24},{8,16},{16,8},{24,0},{1,25},{9,17},{17,9},{25,1},{2,26},{10... | collective-permute-start | bytes 516104 | tf_op jit(solution)/shard_map/ppermute | solution.py:681
  5.6 10.9 %collective-permute-start.7 = (f32[42,8,128]{2,1,0:T(8,128)S(1)}, f32[42,8,128]{2,1,0:T(8,128)S(1)}, u32[]{:S(2)}, u32[]{:S(2)}) collective-permute-start(f32[42,8,128]{2,1,0:T(8,128)S(1)} %get-tuple-element.13.refs_0_), channel_id=1, source_target_pairs={{0,16},{8,24},{16,0},{24,8},{1,17},{9,25},{17,1},{25,9},{2,18},{10... | collective-permute-start | bytes 516104 | tf_op jit(solution)/shard_map/ppermute | solution.py:681
  5.7 5.1 %collective-permute-start.1 = (f32[6,8,128]{2,1,0:T(8,128)S(1)}, f32[6,8,128]{2,1,0:T(8,128)S(1)}, u32[]{:S(2)}, u32[]{:S(2)}) collective-permute-start(f32[6,8,128]{2,1,0:T(8,128)S(1)} %get-tuple-element.12), channel_id=1, source_target_pairs={{0,7},{1,2},{2,1},{3,4},{4,3},{5,6},{6,5},{7,0},{8,15},{9,10},{10,... | collective-permute-start | bytes 73736 | tf_op jit(solution)/shard_map/ppermute | solution.py:681
  10.8 9.2 %collective-permute-start.2 = (f32[12,8,128]{2,1,0:T(8,128)S(1)}, f32[12,8,128]{2,1,0:T(8,128)S(1)}, u32[]{:S(2)}, u32[]{:S(2)}) collective-permute-start(f32[12,8,128]{2,1,0:T(8,128)S(1)} %constant_dynamic-update-slice_fusion.refs_0_), channel_id=1, source_target_pairs={{0,8},{8,0},{16,24},{24,16},{1,9},{9,1},{17,25},{25,17},{2,10},{10... | collective-permute-start | bytes 147464 | tf_op jit(solution)/shard_map/ppermute | solution.py:681
  12.7 7.4 %collective-permute-start.3 = (f32[12,8,128]{2,1,0:T(8,128)S(1)}, f32[12,8,128]{2,1,0:T(8,128)S(1)}, u32[]{:S(2)}, u32[]{:S(2)}) collective-permute-start(f32[12,8,128]{2,1,0:T(8,128)S(1)} %constant_dynamic-update-slice_fusion.refs_0_), channel_id=1, source_target_pairs={{0,24},{8,16},{16,8},{24,0},{1,25},{9,17},{17,9},{25,1},{2,26},{10... | collective-permute-start | bytes 147464 | tf_op jit(solution)/shard_map/ppermute | solution.py:681
  14.2 5.9 %collective-permute-start.4 = (f32[12,8,128]{2,1,0:T(8,128)S(1)}, f32[12,8,128]{2,1,0:T(8,128)S(1)}, u32[]{:S(2)}, u32[]{:S(2)}) collective-permute-start(f32[12,8,128]{2,1,0:T(8,128)S(1)} %constant_dynamic-update-slice_fusion.refs_0_), channel_id=1, source_target_pairs={{0,16},{8,24},{16,0},{24,8},{1,17},{9,25},{17,1},{25,9},{2,18},{10... | collective-permute-start | bytes 147464 | tf_op jit(solution)/shard_map/ppermute | solution.py:681
where the time goes:
time: 24.6 us; the launch traced here: 24.4 us
  starting transfers between devices  11.4 us (46%)
  Pallas kernels  8.91 us (36%)
  waiting for transfers between devices  4.1 us (17%)
    ppermute x8, starting transfers between devices, swapped(): return lax.ppermute(value, axis, list(enumerate(partners)))  11.4 us
    pallas_call x2, Pallas kernels, vmem_call(): pl.pallas_call(kernel, out_shape=out_shapes, in_specs=specs, scratch_shap...  7.87 us
    ppermute x8, waiting for transfers between devices, swapped(): return lax.ppermute(value, axis, list(enumerate(partners)))  4.1 us
    pallas_call x1, Pallas kernels, body_deep(): pl.pallas_call(gather_kernel, out_shape=(planes(42, SUB), border, border))  1.03 us
  transfers between devices with their start and end apart: 8, of which 3 were waited for; matrix products, arithmetic and copies ran while one was open for 0% of the time, Pallas kernels for 14%

commit v1 on v0

--- a/solution.py
+++ b/solution.py
@@ -221,15 +221,19 @@
 SUB = 8
 LANES = 128
 HALF = LANES // 2
-SLOT = 16
 REACH = 2 * ITERS
+SLOT = REACH
 INSIDE = 32 - REACH
 TURN = 2 * REACH
-GROUP = 4
+GROUP = HALF // SLOT
 SIDE_COUNT = -(-21 // GROUP)
 ROWS = 5 * SUB
 FIRST = 2 * SUB
 LAST_ROWS = 2 * SUB
+HALF_TILE = SUB // 2
+FAR_KEPT = REACH - SUB - 1
+FAR_PAD = SUB - 2 * FAR_KEPT
+FAR_FLAGS = -(-(2 * FAR_PAD + 76 * FAR_KEPT) // SUB) * SUB
 PAIRS = [(m, opposite_of(m)) for m in range(1, 19) if m < opposite_of(m)]
 
 
@@ -283,13 +287,38 @@
     return first, second, side
 
 
-def gather_kernel(pop_ref, lab_ref, sol_ref, main, inner_ref, outer_ref):
+def tile_reader(ref):
+    return lambda member, at: ref[2 * member + at]
+
+
+def far_reader(ref):
+    upper = lax.broadcasted_iota(jnp.int32, (SUB, LANES), 0) < HALF_TILE
+
+    def cells(member, at):
+        index = 2 * member + at
+        if member >= 19:
+            return ref[pl.ds(FAR_FLAGS + SUB * (index - 38), SUB), :]
+        first = ref[pl.ds(FAR_PAD + 2 * FAR_KEPT * index, SUB), :]
+        last = ref[pl.ds(FAR_PAD + 2 * FAR_KEPT * (index + 1) - SUB, SUB), :]
+        return jnp.where(upper, first, last)
+
+    return cells
+
+
+def gather_kernel(pop_ref, lab_ref, sol_ref, main, far_ref, inner_ref, outer_ref):
     for member in range(19):
         for at in range(2):
             main[2 * member + at] = pop_ref[member, at]
     for at in range(2):
         main[38 + at] = lab_ref[at].astype(jnp.float32)
         main[40 + at] = sol_ref[at].astype(jnp.float32)
+    for index in range(38):
+        place = FAR_PAD + 2 * FAR_KEPT * index
+        kept = pl.ds(SUB - FAR_KEPT, FAR_KEPT)
+        far_ref[pl.ds(place, FAR_KEPT), :] = pop_ref[index // 2, index % 2, pl.ds(0, FAR_KEPT), :]
+        far_ref[pl.ds(place + FAR_KEPT, FAR_KEPT), :] = pop_ref[index // 2, index % 2, kept, :]
+    for index in range(4):
+        far_ref[pl.ds(FAR_FLAGS + SUB * index, SUB), :] = main[38 + index]
     even = lax.axis_index("gy") % 2 == 0
     low = lane_ids((SUB, LANES)) < HALF
     left_spans = [(SLOT * k, SLOT * k + REACH) for k in range(GROUP)]
@@ -339,9 +368,10 @@
     free = [1, 2, 4, 6, 8] + list(range(9, 19))
     rate = {row: rates_ref[k] * float(1.0 / norms[row]) for k, row in enumerate(free)}
 
-    def put_macro(j, rows, density, reds, where=None):
+    def put_macro(j, rows, density, reds, where=None, sign=None):
         inv = 1.0 / density
-        values = ((total, density), (inverse, inv), (red, reds), (phase, (2.0 * reds - density) * inv))
+        sign = (2.0 * reds - density) * inv if sign is None else sign
+        values = ((total, density), (inverse, inv), (red, reds), (phase, sign))
         for ref, value in values:
             if where is None:
                 ref[j, rows, :] = value
@@ -531,7 +561,7 @@
         for j in range(count):
             rock[j, rows, :] = rocks[j]
             density = weighted_sum(sums[j])
-            put_macro(j, rows, density, labels[j] * density)
+            put_macro(j, rows, density, labels[j] * density, sign=2.0 * labels[j] - 1.0)
 
     def run_early():
         rows_loop(FIRST - REACH + 2, SUB + 2 * REACH - 4, make_masks)
@@ -562,14 +592,15 @@
     deep = (ids >= HALF - INSIDE) & (ids < LANES - INSIDE)
     left = within(shape, (TURN, TURN + INSIDE))
     for source, (main, spots) in enumerate(zip(mains, tile_spots(lax.axis_index("gx"), len(mains)))):
+        read = tile_reader(main) if source < 3 else far_reader(main)
+        cells = [[read(member, 0), read(member, 1)] for member in range(21)]
         for rows in tile_places(spots):
-            labels = [main[38], main[39]]
-            rocks = [main[40], main[41]]
-            stepper.fill(lambda member: [main[2 * member], main[2 * member + 1]], labels, rocks, rows)
+            stepper.fill(lambda member: cells[member], cells[19], cells[20], rows)
         for member in range(21):
-            shallow, below = main[2 * member], main[2 * member + 1]
-            right_part = jnp.where(deep, lane_roll(below, HALF), shallow)
-            left_part = jnp.where(ids < HALF, lane_roll(shallow, TURN), lane_roll(below, HALF + TURN))
+            shallow, below = cells[member]
+            below = lane_roll(below, HALF)
+            right_part = jnp.where(deep, below, shallow)
+            left_part = lane_roll(jnp.where(ids < HALF, shallow, below), TURN)
             zone_ref[source * 21 + member] = jnp.where(left, left_part, right_part)
     stepper.run_early()
     for tile in range(LAST_ROWS // SUB):
@@ -582,7 +613,9 @@
 
 
 def late_kernel(sides, own_ref, rock_ref, zone_ref, rates_ref, out_ref, *scratch):
-    zone_scratch, last_scratch = scratch[:8], scratch[8:]
+    zone_scratch, last_scratch = scratch[:8], scratch[8:16]
+    out_tile, out_sem = scratch[16:]
+    cuts, copies = [6, 12, 18], []
     shape = (SUB, LANES)
     ids = lane_ids(shape)
     sources = zone_ref.shape[0] // 21
@@ -651,7 +684,19 @@
                     bounced = after[19 * s + opposite_of(q), j, rows, :]
                     value = jnp.where(hits[j] > 0.5, bounced, value)
                 value = jnp.where(fluid[j], value, state[19 * s + q, j, rows, :])
-                out_ref[s, q, j] = lane_roll(value, HALF) if j else value
+                out_tile[s, q, j] = lane_roll(value, HALF) if j else value
+        if q in cuts:
+            number = cuts.index(q)
+            first = cuts[number - 1] + 1 if number else 0
+            for s in range(2):
+                part = (s, pl.ds(first, q + 1 - first))
+                copy = pltpu.make_async_copy(
+                    out_tile.at[part], out_ref.at[part], out_sem.at[s, number]
+                )
+                copy.start()
+                copies.append(copy)
+    for copy in copies:
+        copy.wait()
 
 
 def next_pairs(count):
@@ -681,14 +726,17 @@
     return lax.ppermute(value, axis, list(enumerate(partners)))
 
 
-def vmem_call(kernel, out_shapes, args, rates=None, scratch=()):
+def vmem_call(kernel, out_shapes, args, rates=None, scratch=(), out_specs=None):
     vmem = pl.BlockSpec(memory_space=pltpu.VMEM)
     specs = [vmem] * len(args)
     args = [pltpu.with_memory_space_constraint(arg, pltpu.VMEM) for arg in args]
     if rates is not None:
         specs.append(pl.BlockSpec(memory_space=pltpu.SMEM))
         args.append(rates)
-    return pl.pallas_call(kernel, out_shape=out_shapes, in_specs=specs, scratch_shapes=scratch)(*args)
+    kept = {} if out_specs is None else {"out_specs": out_specs}
+    return pl.pallas_call(
+        kernel, out_shape=out_shapes, in_specs=specs, scratch_shapes=scratch, **kept
+    )(*args)
 
 
 def scratch_planes(count, rows):
@@ -713,10 +761,13 @@
         late_kernel(refs[:number], *refs[number:])
 
     border = planes(SIDE_COUNT, SUB)
-    main, inner, outer = pl.pallas_call(gather_kernel, out_shape=(planes(42, SUB), border, border))(
+    shapes = (planes(42, SUB), planes(FAR_FLAGS + 4 * SUB), border, border)
+    main, far, inner, outer = pl.pallas_call(gather_kernel, out_shape=shapes)(
         populations, labels, solid
     )
-    mains = [main] + [swapped(main, "gx", partners) for partners in patterns]
+    mains = [main] + [
+        swapped(main if k < 2 else far, "gx", partners) for k, partners in enumerate(patterns)
+    ]
     outer = swapped(outer, "gy", other_pairs(wide))
     inner = swapped(inner, "gy", next_pairs(wide))
     side = jnp.concatenate([inner, outer], axis=0)
@@ -728,7 +779,10 @@
         jax.ShapeDtypeStruct((2,) + populations.shape, jnp.float32),
         sides + [own, rock, zone],
         rates,
-        scratch_planes(1, ROWS) + scratch_planes(3, LAST_ROWS + SUB),
+        scratch_planes(1, ROWS)
+        + scratch_planes(3, LAST_ROWS + SUB)
+        + [planes(2, 19, 2, SUB), pltpu.SemaphoreType.DMA((2, 3))],
+        pl.BlockSpec(memory_space=pl.ANY),
     )
 
 
@@ -736,7 +790,7 @@
     depth, height, breadth = populations.shape[1:]
     fits = (depth, height, breadth) == (2, SUB, LANES)
     fits = fits and lax.axis_size("gx") % 4 == 0 and lax.axis_size("gy") % 2 == 0
-    if fits and REACH + 2 < SLOT and HALF == 2 * (REACH + INSIDE):
+    if fits and SUB < REACH < 2 * SUB and HALF == 2 * (REACH + INSIDE):
         return body_deep(populations, labels, solid, rates)
     return body_plain(populations, labels, solid, rates)
 

time: 24.6 us -> 23.9 us (0.972)
  waiting for transfers between devices: 4.1 us -> 3.44 us
    ppermute x8, waiting for transfers between devices: 4.1 us -> 3.44 us  [swapped(): return lax.ppermute(value, axis, list(enumerate(partners)))]
  transfers between devices with their start and end apart: 8 -> 8, of which waited for: 3 -> 3; matrix products, arithmetic and copies ran while one was open for 0% -> 0% of each run, Pallas kernels for 14% -> 15%
where the time goes in v1:
time: 23.9 us; the launch traced here: 23.7 us
  starting transfers between devices  11.3 us (47%)
  Pallas kernels  8.88 us (37%)
  waiting for transfers between devices  3.44 us (14%)
    ppermute x8, starting transfers between devices, swapped(): return lax.ppermute(value, axis, list(enumerate(partners)))  11.3 us
    pallas_call x2, Pallas kernels, vmem_call(): pl.pallas_call(kernel, out_shape=out_shapes, in_specs=specs, scratch_shap...  7.82 us
    ppermute x8, waiting for transfers between devices, swapped(): return lax.ppermute(value, axis, list(enumerate(partners)))  3.44 us
    pallas_call x1, Pallas kernels, body_deep(): pl.pallas_call(gather_kernel, out_shape=shapes)(populations, labels, solid)  1.06 us
  transfers between devices with their start and end apart: 8, of which 3 were waited for; matrix products, arithmetic and copies ran while one was open for 0% of the time, Pallas kernels for 15%

profile of v1, /device:TPU:0, one launch (start us, length us, event | category | flops | bytes accessed | tf_op | source)
XLA Modules:
  0.0 23.7 jit_solution(15330415520820839037)
XLA Ops:
  0.0 1.1 %shard_map.46 = (f32[42,8,128]{2,1,0:T(8,128)S(1)}, f32[264,128]{1,0:T(8,128)S(1)}, f32[5,8,128]{2,1,0:T(8,128)S(1)}, f32[5,8,128]{2,1,0:T(8,128)S(1)}) custom-call(f32[19,2,8,128]{3,2,1,0:T(8,128)} %pop_ref.1, s32[2,8,128]{2,1,0:T(8,128)} %lab_ref.1, s32[2,8,128]{2,1,0:T(8,128)} %sol_ref.1), custom_call_target="tpu_custom_call" | custom-call | tf_op jit(solution)/shard_map/pallas_call | solution.py:765
  1.1 0.6 %collective-permute-start = (f32[5,8,128]{2,1,0:T(8,128)S(1)}, f32[5,8,128]{2,1,0:T(8,128)S(1)}, u32[]{:S(2)}, u32[]{:S(2)}) collective-permute-start(f32[5,8,128]{2,1,0:T(8,128)S(1)} %get-tuple-element.12), channel_id=1, source_target_pairs={{0,1},{1,0},{2,3},{3,2},{4,5},{5,4},{6,7},{7,6},{8,9},{9,8},{10,11... | collective-permute-start | bytes 61448 | tf_op jit(solution)/shard_map/ppermute | solution.py:726
  1.6 2.6 %collective-permute-start.5 = (f32[42,8,128]{2,1,0:T(8,128)S(1)}, f32[42,8,128]{2,1,0:T(8,128)S(1)}, u32[]{:S(2)}, u32[]{:S(2)}) collective-permute-start(f32[42,8,128]{2,1,0:T(8,128)S(1)} %get-tuple-element.14.refs_0_), channel_id=1, source_target_pairs={{0,8},{8,0},{16,24},{24,16},{1,9},{9,1},{17,25},{25,17},{2,10},{10... | collective-permute-start | bytes 516104 | tf_op jit(solution)/shard_map/ppermute | solution.py:726
  4.2 1.5 %collective-permute-start.6 = (f32[42,8,128]{2,1,0:T(8,128)S(1)}, f32[42,8,128]{2,1,0:T(8,128)S(1)}, u32[]{:S(2)}, u32[]{:S(2)}) collective-permute-start(f32[42,8,128]{2,1,0:T(8,128)S(1)} %get-tuple-element.14.refs_0_), channel_id=1, source_target_pairs={{0,24},{8,16},{16,8},{24,0},{1,25},{9,17},{17,9},{25,1},{2,26},{10... | collective-permute-start | bytes 516104 | tf_op jit(solution)/shard_map/ppermute | solution.py:726
  5.7 0.1 collective-permute-start.7
  5.7 3.3 %collective-permute-start.1 = (f32[5,8,128]{2,1,0:T(8,128)S(1)}, f32[5,8,128]{2,1,0:T(8,128)S(1)}, u32[]{:S(2)}, u32[]{:S(2)}) collective-permute-start(f32[5,8,128]{2,1,0:T(8,128)S(1)} %get-tuple-element.13), channel_id=1, source_target_pairs={{0,7},{1,2},{2,1},{3,4},{4,3},{5,6},{6,5},{7,0},{8,15},{9,10},{10,... | collective-permute-start | bytes 61448 | tf_op jit(solution)/shard_map/ppermute | solution.py:726
  9.0 0.0 collective-permute-done
  9.0 1.8 %collective-permute-done.1 = f32[5,8,128]{2,1,0:T(8,128)S(1)} collective-permute-done((f32[5,8,128]{2,1,0:T(8,128)S(1)}, f32[5,8,128]{2,1,0:T(8,128)S(1)}, u32[]{:S(2)}, u32[]{:S(2)}) %collective-permute-start.1) | collective-permute-done | bytes 20512 | tf_op jit(solution)/shard_map/ppermute | solution.py:726
  10.8 1.9 %collective-permute-start.2 = (f32[10,8,128]{2,1,0:T(8,128)S(1)}, f32[10,8,128]{2,1,0:T(8,128)S(1)}, u32[]{:S(2)}, u32[]{:S(2)}) collective-permute-start(f32[10,8,128]{2,1,0:T(8,128)S(1)} %constant_dynamic-update-slice_fusion.refs_0_), channel_id=1, source_target_pairs={{0,8},{8,0},{16,24},{24,16},{1,9},{9,1},{17,25},{25,17},{2,10},{10... | collective-permute-start | bytes 122888 | tf_op jit(solution)/shard_map/ppermute | solution.py:726
  12.7 1.5 %collective-permute-start.3 = (f32[10,8,128]{2,1,0:T(8,128)S(1)}, f32[10,8,128]{2,1,0:T(8,128)S(1)}, u32[]{:S(2)}, u32[]{:S(2)}) collective-permute-start(f32[10,8,128]{2,1,0:T(8,128)S(1)} %constant_dynamic-update-slice_fusion.refs_0_), channel_id=1, source_target_pairs={{0,24},{8,16},{16,8},{24,0},{1,25},{9,17},{17,9},{25,1},{2,26},{10... | collective-permute-start | bytes 122888 | tf_op jit(solution)/shard_map/ppermute | solution.py:726
  14.2 1.2 %collective-permute-done.7.refs_3_ = f32[264,128]{1,0:T(8,128)S(1)} collective-permute-done((f32[264,128]{1,0:T(8,128)S(1)}, f32[264,128]{1,0:T(8,128)S(1)}, u32[]{:S(2)}, u32[]{:S(2)}) %collective-permute-start.7) | collective-permute-done | bytes 135200 | tf_op jit(solution)/shard_map/ppermute | solution.py:726
  15.4 0.0 collective-permute-start.4
  15.4 0.0 collective-permute-done.5.refs_1_
  15.4 0.0 collective-permute-done.6.refs_2_
  15.4 3.5 %shard_map.47 = (f32[38,2,16,128]{3,2,1,0:T(8,128)S(1)}, f32[2,16,128]{2,1,0:T(8,128)S(1)}, f32[84,8,128]{2,1,0:T(8,128)S(1)}) custom-call(f32[42,8,128]{2,1,0:T(8,128)S(1)} %get-tuple-element.14.refs_0_, f32[42,8,128]{2,1,0:T(8,128)S(1)} %collective-permute-done.5.refs_1_, f32[42,8,128]{2,1,0:T(8,128)S(1)} %collective-permute-done.6.refs_2_, ...), custom_call_target="tpu_custom_call" | custom-call | tf_op jit(solution)/shard_map/pallas_call | solution.py:737
  18.8 0.0 collective-permute-done.2.refs_1_
  18.9 0.0 collective-permute-done.3.refs_2_
  18.9 0.5 %collective-permute-done.4.refs_3_ = f32[10,8,128]{2,1,0:T(8,128)S(1)} collective-permute-done((f32[10,8,128]{2,1,0:T(8,128)S(1)}, f32[10,8,128]{2,1,0:T(8,128)S(1)}, u32[]{:S(2)}, u32[]{:S(2)}) %collective-permute-start.4) | collective-permute-done | bytes 40992 | tf_op jit(solution)/shard_map/ppermute | solution.py:726
  19.4 4.3 %shard_map.48 = f32[2,19,2,8,128]{4,3,2,1,0:T(8,128)} custom-call(f32[10,8,128]{2,1,0:T(8,128)S(1)} %constant_dynamic-update-slice_fusion.refs_0_, f32[10,8,128]{2,1,0:T(8,128)S(1)} %collective-permute-done.2.refs_1_, f32[10,8,128]{2,1,0:T(8,128)S(1)} %collective-permute-done.3.refs_2_, f32[10,8,128]{2,1,0:T(8,128)S(1)} %collective-permute-done.4.refs_3_, ...), custom_call_target="tpu_custom_call" | custom-call | tf_op jit(solution)/shard_map/pallas_call | solution.py:737
  (2 shorter events, 0.0 us)
Async XLA Ops:
  1.1 7.9 %collective-permute-start = (f32[5,8,128]{2,1,0:T(8,128)S(1)}, f32[5,8,128]{2,1,0:T(8,128)S(1)}, u32[]{:S(2)}, u32[]{:S(2)}) collective-permute-start(f32[5,8,128]{2,1,0:T(8,128)S(1)} %get-tuple-element.12), channel_id=1, source_target_pairs={{0,1},{1,0},{2,3},{3,2},{4,5},{5,4},{6,7},{7,6},{8,9},{9,8},{10,11... | collective-permute-start | bytes 61448 | tf_op jit(solution)/shard_map/ppermute | solution.py:726
  1.6 13.7 %collective-permute-start.5 = (f32[42,8,128]{2,1,0:T(8,128)S(1)}, f32[42,8,128]{2,1,0:T(8,128)S(1)}, u32[]{:S(2)}, u32[]{:S(2)}) collective-permute-start(f32[42,8,128]{2,1,0:T(8,128)S(1)} %get-tuple-element.14.refs_0_), channel_id=1, source_target_pairs={{0,8},{8,0},{16,24},{24,16},{1,9},{9,1},{17,25},{25,17},{2,10},{10... | collective-permute-start | bytes 516104 | tf_op jit(solution)/shard_map/ppermute | solution.py:726
  4.2 11.2 %collective-permute-start.6 = (f32[42,8,128]{2,1,0:T(8,128)S(1)}, f32[42,8,128]{2,1,0:T(8,128)S(1)}, u32[]{:S(2)}, u32[]{:S(2)}) collective-permute-start(f32[42,8,128]{2,1,0:T(8,128)S(1)} %get-tuple-element.14.refs_0_), channel_id=1, source_target_pairs={{0,24},{8,16},{16,8},{24,0},{1,25},{9,17},{17,9},{25,1},{2,26},{10... | collective-permute-start | bytes 516104 | tf_op jit(solution)/shard_map/ppermute | solution.py:726
  5.7 9.7 %collective-permute-start.7 = (f32[264,128]{1,0:T(8,128)S(1)}, f32[264,128]{1,0:T(8,128)S(1)}, u32[]{:S(2)}, u32[]{:S(2)}) collective-permute-start(f32[264,128]{1,0:T(8,128)S(1)} %get-tuple-element.15), channel_id=1, source_target_pairs={{0,16},{8,24},{16,0},{24,8},{1,17},{9,25},{17,1},{25,9},{2,18},{10... | collective-permute-start | bytes 405512 | tf_op jit(solution)/shard_map/ppermute | solution.py:726
  5.7 5.0 %collective-permute-start.1 = (f32[5,8,128]{2,1,0:T(8,128)S(1)}, f32[5,8,128]{2,1,0:T(8,128)S(1)}, u32[]{:S(2)}, u32[]{:S(2)}) collective-permute-start(f32[5,8,128]{2,1,0:T(8,128)S(1)} %get-tuple-element.13), channel_id=1, source_target_pairs={{0,7},{1,2},{2,1},{3,4},{4,3},{5,6},{6,5},{7,0},{8,15},{9,10},{10,... | collective-permute-start | bytes 61448 | tf_op jit(solution)/shard_map/ppermute | solution.py:726
  10.8 8.1 %collective-permute-start.2 = (f32[10,8,128]{2,1,0:T(8,128)S(1)}, f32[10,8,128]{2,1,0:T(8,128)S(1)}, u32[]{:S(2)}, u32[]{:S(2)}) collective-permute-start(f32[10,8,128]{2,1,0:T(8,128)S(1)} %constant_dynamic-update-slice_fusion.refs_0_), channel_id=1, source_target_pairs={{0,8},{8,0},{16,24},{24,16},{1,9},{9,1},{17,25},{25,17},{2,10},{10... | collective-permute-start | bytes 122888 | tf_op jit(solution)/shard_map/ppermute | solution.py:726
  12.7 6.2 %collective-permute-start.3 = (f32[10,8,128]{2,1,0:T(8,128)S(1)}, f32[10,8,128]{2,1,0:T(8,128)S(1)}, u32[]{:S(2)}, u32[]{:S(2)}) collective-permute-start(f32[10,8,128]{2,1,0:T(8,128)S(1)} %constant_dynamic-update-slice_fusion.refs_0_), channel_id=1, source_target_pairs={{0,24},{8,16},{16,8},{24,0},{1,25},{9,17},{17,9},{25,1},{2,26},{10... | collective-permute-start | bytes 122888 | tf_op jit(solution)/shard_map/ppermute | solution.py:726
  15.4 4.0 %collective-permute-start.4 = (f32[10,8,128]{2,1,0:T(8,128)S(1)}, f32[10,8,128]{2,1,0:T(8,128)S(1)}, u32[]{:S(2)}, u32[]{:S(2)}) collective-permute-start(f32[10,8,128]{2,1,0:T(8,128)S(1)} %constant_dynamic-update-slice_fusion.refs_0_), channel_id=1, source_target_pairs={{0,16},{8,24},{16,0},{24,8},{1,17},{9,25},{17,1},{25,9},{2,18},{10... | collective-permute-start | bytes 122888 | tf_op jit(solution)/shard_map/ppermute | solution.py:726
